TPU v7x, 32 devices: a whole 2x2x4 slice. The times are simulated.
32 devices in a mesh: cfg: 2 (over y), space: 8 (over z, x), tm: 2 (over core).
Axes of the slice: x: 2, y: 2, z: 4, core: 2. Of those that a mesh axis runs over, the one named last changes fastest.
Arguments:
- eigvecs: bfloat16 [4, 2, 3, 1536, 256], P(('cfg', 'tm'), None, None, 'space'), parts along dimension 0, may hold values from -6 to 6
- momenta: int32 [3, 3], replicated, may hold values from -2 to 2, as said below
- pair_list: int32 [8, 2], P('tm'), may hold values from 0 to 1
- panels: bfloat16 [16, 2, 1024, 1024], P(('cfg', 'tm'), None, 'space'), parts along dimension 0, may hold values from -6 to 6
Outputs:
- dressed: bfloat16 [16, 3, 2, 1024, 1024], P(('cfg', 'tm'), None, None, 'space'), parts along dimension 0
There are 2 independent parts, one for each index of `cfg`. A program takes and returns all parts, laid end to end along the dimension named above; an argument that names none is the same for every part. Nothing has to cross between parts.
Inputs may be any that keep to these rules, and one draw needn't show every extreme that they name: `momenta`: the first component of every momentum is nonzero.
All inputs are finite; a program needn't handle non-finite values.
Results may differ from a plain program's by a relative error of at most 0.0075.
Values may be sent and summed in bfloat16 or wider, within the bound.
A program may use at most 64 MiB of HBM per device.

v0:
```python
import math
import jax
import jax.numpy as jnp
from jax import lax
from jax.sharding import PartitionSpec as P

LX = 64


def phased_block(cosine, sine_part, real_part, imag_part):
    cos_col = cosine[:, None]
    sin_col = sine_part[:, None]
    wave_re = cos_col * real_part + sin_col * imag_part
    wave_im = cos_col * imag_part - sin_col * real_part
    upper = jnp.concatenate([wave_re, wave_im], -1)
    lower = jnp.concatenate([wave_im, -wave_re], -1)
    return jnp.stack([upper, lower], -4).astype(jnp.bfloat16)


def local(eigvecs, momenta, pair_list, panels):
    slice_count, _, colors, slab_sites, vectors = eigvecs.shape
    mom_count = momenta.shape[0]
    space_count = lax.axis_size("space")
    first_site = lax.axis_index("space") * slab_sites
    site_index = first_site + jnp.arange(slab_sites, dtype=jnp.int32)
    xpos = site_index % LX
    ypos = site_index // LX % LX
    zpos = site_index // (LX * LX)
    wave = (
        momenta[:, 0:1] * xpos[None, :]
        + momenta[:, 1:2] * ypos[None, :]
        + momenta[:, 2:3] * zpos[None, :]
    )
    wave = jnp.mod(wave, LX)
    angle = wave.astype(jnp.float32) * jnp.float32(2.0 * math.pi / LX)
    cosine = jnp.cos(angle)
    sine_part = jnp.sin(angle)
    factor = 1.0 / math.sqrt(6.0 * slab_sites * space_count * vectors)
    real_part = eigvecs[:, 0].astype(jnp.float32)
    imag_part = eigvecs[:, 1].astype(jnp.float32)
    phased_all = jnp.concatenate(
        [
            phased_block(cosine[moment], sine_part[moment], real_part, imag_part)
            for moment in range(mom_count)
        ],
        -1,
    )
    phased_all = phased_all.reshape(slice_count, 2, colors, slab_sites, mom_count, 2 * vectors)
    gram_local = jnp.einsum(
        "trcsk,trcsml->tmkl", eigvecs, phased_all, preferred_element_type=jnp.float32
    )
    gram_local = factor * gram_local
    summed = lax.psum(gram_local, "space")
    own_fields = summed.astype(jnp.bfloat16)
    meson_fields = lax.all_gather(own_fields, "tm", axis=0, tiled=True)
    pair_count = pair_list.shape[0]
    panel_rows = panels.shape[2]
    panel_width = panels.shape[3]
    spins = panel_width // vectors
    source_fields = jnp.take(meson_fields, pair_list[:, 0], axis=0).reshape(
        pair_count, mom_count, vectors, 2, vectors
    )
    sink_fields = jnp.take(meson_fields, pair_list[:, 1], axis=0).reshape(
        pair_count, mom_count, vectors, 2, vectors
    )
    panel_parts = panels.reshape(pair_count, 2, panel_rows, spins, vectors)
    panel_re = panel_parts[:, 0]
    panel_im = panel_parts[:, 1]
    panel_mix = jnp.stack(
        [jnp.stack([panel_re, panel_im], 1), jnp.stack([panel_im, -panel_re], 1)], 1
    )
    right_dressed = jnp.einsum(
        "porxbk,pmlrk->pmoxbl", panel_mix, source_fields, preferred_element_type=jnp.float32
    )
    right_dressed = right_dressed.astype(jnp.bfloat16).reshape(
        pair_count * mom_count, 2, panel_rows, panel_width
    )
    turned = lax.all_to_all(right_dressed, "space", split_axis=3, concat_axis=2, tiled=True)
    column_count = turned.shape[3]
    turned = turned.reshape(pair_count, mom_count, 2, spins, vectors, column_count)
    turned_re = turned[:, :, 0]
    turned_im = turned[:, :, 1]
    mixed_parts = jnp.stack(
        [jnp.stack([turned_re, -turned_im], 2), jnp.stack([turned_im, turned_re], 2)], 2
    )
    dressed = jnp.einsum(
        "pmorajc,pmkrj->pmocak", mixed_parts, sink_fields, preferred_element_type=jnp.float32
    )
    return dressed.reshape(pair_count, mom_count, 2, column_count, panel_width).astype(jnp.bfloat16)


def solution(mesh):
    placed = (
        P(("cfg", "tm"), None, None, "space", None),
        P(),
        P("tm", None),
        P(("cfg", "tm"), None, "space", None),
    )
    return jax.shard_map(
        local,
        mesh=mesh,
        in_specs=placed,
        out_specs=P(("cfg", "tm"), None, None, "space", None),
        check_vma=False,
    )
```

profile of v0, /device:TPU:0, one launch (start us, length us, event | category | flops | bytes accessed | tf_op | source)
XLA Modules:
  0.0 343.8 jit_solution(5193341892418195743)
XLA Ops:
  6.5 0.0 all-gather.2.cloned.1.call-start
  6.6 1.0 slice_reduce_fusion.2
  7.6 0.1 fusion.37
  7.7 0.0 copy-start.3
  7.8 1.6 fusion.30
  9.3 0.1 maximum_bitcast_fusion.9
  9.4 0.1 pad_maximum_fusion
  9.5 0.0 copy-done.3
  9.6 0.3 fusion.28
  9.8 0.1 maximum_bitcast_fusion.11
  10.0 0.1 maximum_bitcast_fusion.13
  10.1 1.2 fusion.17
  11.3 83.3 %all-reduce.1 = bf16[1,3,256,512]{2,3,1,0:T(8,128)(2,1)S(1)} all-reduce(f32[1,3,256,512]{2,3,1,0:T(8,128)S(1)} %fusion.17), channel_id=1, replica_groups=mesh['cfg'=2,'space'=8,'tm'=2] {'space'}, use_global_device_ids=true, to_apply=%region_0.1 | all-reduce | flops 393216 | bytes 2359296 | tf_op jit(solution)/shard_map/psum | solution.py:53
  94.7 1.3 copy.48
  95.9 0.0 all-gather.2.cloned.1.call-update
  95.9 3.0 copy.49
  99.0 1.5 fusion.42
  100.4 1.5 copy.77
  102.0 1.2 neg.44
  103.2 0.0 copy-start.4
  103.2 0.0 copy-start.2
  103.2 2.4 copy.76
  105.6 2.3 copy.53
  107.9 0.0 copy-done.4
  107.9 0.0 copy-done.2
  107.9 2.7 maximum_bitcast_fusion.6
  110.7 0.0 all-gather.2.cloned.1.call-done
  110.7 2.2 gather_fusion.1
  112.8 2.0 broadcast_select_fusion
  114.9 3.8 %reshape.415 = bf16[4,3,256,2,256]{4,3,2,1,0:T(2,128)(2,1)S(1)} reshape(bf16[4,3,256,512]{3,2,1,0:T(8,128)(2,1)} %broadcast_select_fusion) | data formatting | bytes 6291456 | tf_op jit(solution)/shard_map/reshape | solution.py:60
  118.6 6.2 %bitcast_convert_fusion.1 = bf16[4,3,256,2,128,4]{4,2,5,3,1,0:T(8,128)(2,1)S(1)} fusion(bf16[4,1,2,128,4,256]{5,3,2,4,1,0:T(8,128)(2,1)} %maximum_bitcast_fusion.6, bf16[4,1,2,128,4,256]{5,3,2,4,1,0:T(8,128)(2,1)} %copy.53, bf16[4,3,256,2,256,1,1]{4,3,2,1,0,6,5:T(2,128)(2,1)S(1)} %bitcast.120), kind=kOutput, calls=%fused_computation.7 | convolution fusion | flops 3232759808 | bytes 13631488 | tf_op jit(solution)/shard_map/porxbk,pmlrk->pmoxbl/dot_general | solution.py:72
  124.8 36.6 %copy.55 = bf16[12,2,128,1024]{2,1,0,3:T(2,128)(2,1)} copy(bf16[12,2,128,1024]{2,3,1,0:T(8,128)(2,1)S(1)} %bitcast.117) | data formatting | bytes 12582912 | tf_op jit(solution)/shard_map/reshape | solution.py:75
  161.5 0.0 copy-start.1
  161.5 5.1 %all-to-all-start = ((bf16[12,2,128,1024]{2,1,0,3:T(2,128)(2,1)}), bf16[12,2,128,1024]{2,1,0,3:T(2,128)(2,1)}, u32[]{:S(2)}, u32[]{:S(2)}) async-start(bf16[12,2,128,1024]{2,1,0,3:T(2,128)(2,1)} %copy.55), calls=%async_computation | async-start | bytes 12582912 | tf_op jit(solution)/shard_map/all_to_all | solution.py:78
  166.5 0.0 copy-done.1
  166.6 2.5 gather_fusion
  169.0 2.3 broadcast_select_fusion.1
  171.3 3.1 reshape.414
  174.3 125.2 %all-to-all-done = bf16[12,2,128,1024]{2,1,0,3:T(2,128)(2,1)} async-done(((bf16[12,2,128,1024]{2,1,0,3:T(2,128)(2,1)}), bf16[12,2,128,1024]{2,1,0,3:T(2,128)(2,1)}, u32[]{:S(2)}, u32[]{:S(2)}) %all-to-all-start) | async-done | bytes 6291488 | tf_op jit(solution)/shard_map/all_to_all | solution.py:78
  299.6 6.9 %copy.56 = bf16[12,2,128,1024]{2,3,1,0:T(8,128)(2,1)} copy(bf16[12,2,128,1024]{2,1,0,3:T(2,128)(2,1)} %all-to-all-done) | data formatting | bytes 12582912 | tf_op jit(solution)/shard_map/all_to_all | solution.py:78
  306.4 8.6 %copy.57 = bf16[12,2,8,128,128]{4,3,2,1,0:T(8,128)(2,1)} copy(bf16[12,2,8,128,128]{3,4,2,1,0:T(8,128)(2,1)} %bitcast.114) | data formatting | bytes 12582912 | tf_op jit(solution)/shard_map/all_to_all | solution.py:78
  315.1 0.0 copy-start
  315.1 3.4 slice_bitcast_fusion
  318.5 1.2 copy-done
  319.7 0.4 fusion.41
  320.1 1.0 maximum_bitcast_fusion
  321.1 7.2 %bitcast_convert_fusion = bf16[4,3,256,2,4,128]{5,2,4,3,1,0:T(8,128)(2,1)} fusion(bf16[4,3,1,2,4,256,128]{6,5,3,4,2,1,0:T(8,128)(2,1)S(1)} %get-tuple-element.16, bf16[4,3,1,2,4,256,128]{6,5,3,4,2,1,0:T(8,128)(2,1)S(1)} %get-tuple-element.15, bf16[4,3,256,2,256,1,1]{4,3,2,1,0,6,5:T(2,128)(2,1)} %bitcast.119), kind=kOutput, calls=%fused_computation.6 | convolution fusion | flops 3249537024 | bytes 22020096 | tf_op jit(solution)/shard_map/pmorajc,pmkrj->pmocak/dot_general | solution.py:86
  328.3 8.6 %copy.62 = bf16[4,3,2,128,1024]{4,3,2,1,0:T(8,128)(2,1)} copy(bf16[4,3,2,128,1024]{3,4,2,1,0:T(8,128)(2,1)} %bitcast.118) | data formatting | bytes 12582912 | tf_op jit(solution)/shard_map/convert_element_type | solution.py:89
  (6 shorter events, 0.1 us)
Async XLA Ops:
  6.5 104.1 %all-gather.2.cloned.1.call-start = ((), (), s32[]{:S(2)}) async-start(), calls=%async_computation.1 | async-start | bytes 2359296 | tf_op jit(solution)/shard_map/all_gather | solution.py:55
  7.7 1.8 copy-start.3
  103.2 4.7 %copy-start.4 = (s32[4,2]{0,1:T(2,128)S(1)}, s32[4,2]{0,1:T(2,128)}, u32[]{:S(2)}) copy-start(s32[4,2]{0,1:T(2,128)} %param.8) | copy-start | bytes 100
  103.2 4.7 %copy-start.2 = (bf16[4,1,128,4,256]{4,2,1,3,0:T(8,128)(2,1)S(1)}, bf16[4,1,128,4,256]{4,2,1,3,0:T(8,128)(2,1)}, u32[]{:S(2)}) copy-start(bf16[4,1,128,4,256]{4,2,1,3,0:T(8,128)(2,1)} %neg.44) | copy-start | bytes 3145732
  161.5 5.1 %copy-start.1 = (bf16[2,3,256,512]{3,2,1,0:T(8,128)(2,1)S(1)}, bf16[2,3,256,512]{3,2,1,0:T(8,128)(2,1)}, u32[]{:S(2)}) copy-start(bf16[2,3,256,512]{3,2,1,0:T(8,128)(2,1)} %all-gather.2.cloned.1.call-done) | copy-start | bytes 4718596
  161.5 138.1 %all-to-all-start = ((bf16[12,2,128,1024]{2,1,0,3:T(2,128)(2,1)}), bf16[12,2,128,1024]{2,1,0,3:T(2,128)(2,1)}, u32[]{:S(2)}, u32[]{:S(2)}) async-start(bf16[12,2,128,1024]{2,1,0,3:T(2,128)(2,1)} %copy.55), calls=%async_computation | async-start | bytes 12582912 | tf_op jit(solution)/shard_map/all_to_all | solution.py:78
  315.1 4.6 %copy-start = (bf16[12,2,8,128,128]{4,3,2,1,0:T(8,128)(2,1)S(1)}, bf16[12,2,8,128,128]{4,3,2,1,0:T(8,128)(2,1)}, u32[]{:S(2)}) copy-start(bf16[12,2,8,128,128]{4,3,2,1,0:T(8,128)(2,1)} %copy.57) | copy-start | bytes 18874372
Sparse Core Ops, SparseCore 0:
  96.1 7.9 all-gather.1
where the time goes:
time: 345 us; the launch traced here: 344 us
  waiting for transfers between devices  125 us (36%)
  local copies, waits for them, and re-layouts  89.8 us (26%)
  blocking collectives  83.3 us (24%)
  matrix products  14.6 us (4%)
  between operations  13.6 us (4%)
  other arithmetic  12 us (3%)
  starting transfers between devices  5.08 us (1%)
    all_to_all x1, waiting for transfers between devices, local(): lax.all_to_all(right_dressed, 'space', split_axis=3, concat_axis=2, tiled...  125 us
    psum x1, blocking collectives, local(): summed = lax.psum(gram_local, 'space')  83.3 us
    reshape x1, local copies, waits for them, and re-layouts, local(): right_dressed.astype(jnp.bfloat16)  36.6 us
    all_to_all x2, local copies, waits for them, and re-layouts, local(): lax.all_to_all(right_dressed, 'space', split_axis=3, concat_axis=2, tiled...  15.5 us
    unnamed x14, local copies, waits for them, and re-layouts  11.6 us
    convert_element_type x1, local copies, waits for them, and re-layouts, local(): dressed.reshape(pair_count, mom_count, 2, column_count, panel_width)  8.62 us
    dot_general x1, matrix products, local(): jnp.einsum('pmorajc,pmkrj->pmocak', mixed_parts, sink_fields, preferred_e...  7.2 us
  transfers between devices with their start and end apart: 2, of which 1 were waited for; matrix products, arithmetic and copies ran while one was open for 7% of the time, Pallas kernels for 0%

commit v1 on v0

--- a/solution.py
+++ b/solution.py
@@ -50,7 +50,9 @@
         "trcsk,trcsml->tmkl", eigvecs, phased_all, preferred_element_type=jnp.float32
     )
     gram_local = factor * gram_local
-    summed = lax.psum(gram_local, "space")
+    summed = gram_local
+    for hop in (1, 2, 4):
+        summed = summed + lax.ppermute(summed, "space", [(dev, dev ^ hop) for dev in range(8)])
     own_fields = summed.astype(jnp.bfloat16)
     meson_fields = lax.all_gather(own_fields, "tm", axis=0, tiled=True)
     pair_count = pair_list.shape[0]

time: 345 us -> 410 us (1.19)
  waiting for transfers between devices: 125 us -> 266 us
  blocking collectives: 83.3 us -> 0 us
  starting transfers between devices: 5.08 us -> 13 us
    ppermute x0 -> x3, waiting for transfers between devices: none -> 135 us  [local(): lax.ppermute(summed, 'space', [(dev, dev ^ hop) for dev in range(8)])]
    psum x1 -> x0, blocking collectives: 83.3 us -> none  [local(): summed = lax.psum(gram_local, 'space')]
    ppermute x0 -> x3, starting transfers between devices: none -> 7.54 us  [local(): lax.ppermute(summed, 'space', [(dev, dev ^ hop) for dev in range(8)])]
    all_to_all x1, waiting for transfers between devices: 125 us -> 131 us  [local(): lax.all_to_all(right_dressed, 'space', split_axis=3, concat_axis=2, tiled...]
  transfers between devices with their start and end apart: 2 -> 5, of which waited for: 1 -> 4; matrix products, arithmetic and copies ran while one was open for 7% -> 6% of each run, Pallas kernels for 0% -> 0%
where the time goes in v1:
time: 410 us; the launch traced here: 409 us
  waiting for transfers between devices  266 us (65%)
  local copies, waits for them, and re-layouts  89.9 us (22%)
  matrix products  14.6 us (4%)
  between operations  13.6 us (3%)
  starting transfers between devices  13 us (3%)
  other arithmetic  12.7 us (3%)
    ppermute x3, waiting for transfers between devices, local(): lax.ppermute(summed, 'space', [(dev, dev ^ hop) for dev in range(8)])  135 us
    all_to_all x1, waiting for transfers between devices, local(): lax.all_to_all(right_dressed, 'space', split_axis=3, concat_axis=2, tiled...  131 us
    reshape x1, local copies, waits for them, and re-layouts, local(): right_dressed.astype(jnp.bfloat16)  36.6 us
    all_to_all x2, local copies, waits for them, and re-layouts, local(): lax.all_to_all(right_dressed, 'space', split_axis=3, concat_axis=2, tiled...  15.6 us
    unnamed x14, local copies, waits for them, and re-layouts  11.6 us
    convert_element_type x1, local copies, waits for them, and re-layouts, local(): dressed.reshape(pair_count, mom_count, 2, column_count, panel_width)  8.62 us
  transfers between devices with their start and end apart: 5, of which 4 were waited for; matrix products, arithmetic and copies ran while one was open for 6% of the time, Pallas kernels for 0%

profile of v1, /device:TPU:0, one launch (start us, length us, event | category | flops | bytes accessed | tf_op | source)
XLA Modules:
  0.0 409.4 jit_solution(398115430253767199)
XLA Ops:
  6.5 0.0 all-gather.2.cloned.1.call-start
  6.6 1.0 slice_reduce_fusion.2
  7.6 0.1 fusion.37
  7.7 0.0 copy-start.3
  7.8 1.6 fusion.30
  9.3 0.1 maximum_bitcast_fusion.9
  9.4 0.1 pad_maximum_fusion
  9.5 0.0 copy-done.3
  9.6 0.3 fusion.28
  9.8 0.1 maximum_bitcast_fusion.11
  10.0 0.1 maximum_bitcast_fusion.13
  10.1 1.2 fusion.17
  11.3 3.0 collective-permute-start
  14.3 34.4 %collective-permute-done = f32[1,3,256,512]{2,3,1,0:T(8,128)S(1)} collective-permute-done((f32[1,3,256,512]{2,3,1,0:T(8,128)S(1)}, f32[1,3,256,512]{2,3,1,0:T(8,128)S(1)}, u32[]{:S(2)}, u32[]{:S(2)}) %collective-permute-start) | collective-permute-done | bytes 1572896 | tf_op jit(solution)/shard_map/ppermute | solution.py:55
  48.7 0.2 add.123
  48.9 1.9 collective-permute-start.1
  50.8 33.7 %collective-permute-done.1 = f32[1,3,256,512]{2,3,1,0:T(8,128)S(1)} collective-permute-done((f32[1,3,256,512]{2,3,1,0:T(8,128)S(1)}, f32[1,3,256,512]{2,3,1,0:T(8,128)S(1)}, u32[]{:S(2)}, u32[]{:S(2)}) %collective-permute-start.1) | collective-permute-done | bytes 1572896 | tf_op jit(solution)/shard_map/ppermute | solution.py:55
  84.6 0.2 add.124
  84.8 2.6 collective-permute-start.2
  87.4 66.8 %collective-permute-done.2 = f32[1,3,256,512]{2,3,1,0:T(8,128)S(1)} collective-permute-done((f32[1,3,256,512]{2,3,1,0:T(8,128)S(1)}, f32[1,3,256,512]{2,3,1,0:T(8,128)S(1)}, u32[]{:S(2)}, u32[]{:S(2)}) %collective-permute-start.2) | collective-permute-done | bytes 1572896 | tf_op jit(solution)/shard_map/ppermute | solution.py:55
  154.1 0.3 add_convert_fusion
  154.4 1.2 copy.48
  155.7 0.0 all-gather.2.cloned.1.call-update
  155.7 3.0 copy.49
  158.7 1.5 fusion.42
  160.2 1.5 copy.77
  161.7 1.2 neg.44
  162.9 2.4 copy.76
  165.3 2.4 copy.53
  167.8 2.7 maximum_bitcast_fusion.6
  170.5 2.2 gather_fusion.1
  172.7 2.0 broadcast_select_fusion
  174.7 3.8 reshape.415
  178.5 6.2 %bitcast_convert_fusion.1 = bf16[4,3,256,2,128,4]{4,2,5,3,1,0:T(8,128)(2,1)S(1)} fusion(bf16[4,1,2,128,4,256]{5,3,2,4,1,0:T(8,128)(2,1)} %maximum_bitcast_fusion.6, bf16[4,1,2,128,4,256]{5,3,2,4,1,0:T(8,128)(2,1)} %copy.53, bf16[4,3,256,2,256,1,1]{4,3,2,1,0,6,5:T(2,128)(2,1)S(1)} %bitcast.120), kind=kOutput, calls=%fused_computation.7 | convolution fusion | flops 3232759808 | bytes 13631488 | tf_op jit(solution)/shard_map/porxbk,pmlrk->pmoxbl/dot_general | solution.py:74
  184.7 36.6 %copy.55 = bf16[12,2,128,1024]{2,1,0,3:T(2,128)(2,1)} copy(bf16[12,2,128,1024]{2,3,1,0:T(8,128)(2,1)S(1)} %bitcast.117) | data formatting | bytes 12582912 | tf_op jit(solution)/shard_map/reshape | solution.py:77
  221.3 5.5 %all-to-all-start = ((bf16[12,2,128,1024]{2,1,0,3:T(2,128)(2,1)}), bf16[12,2,128,1024]{2,1,0,3:T(2,128)(2,1)}, u32[]{:S(2)}, u32[]{:S(2)}) async-start(bf16[12,2,128,1024]{2,1,0,3:T(2,128)(2,1)} %copy.55), calls=%async_computation | async-start | bytes 12582912 | tf_op jit(solution)/shard_map/all_to_all | solution.py:80
  226.8 2.5 gather_fusion
  229.2 2.3 broadcast_select_fusion.1
  231.5 3.1 reshape.414
  234.6 130.6 %all-to-all-done = bf16[12,2,128,1024]{2,1,0,3:T(2,128)(2,1)} async-done(((bf16[12,2,128,1024]{2,1,0,3:T(2,128)(2,1)}), bf16[12,2,128,1024]{2,1,0,3:T(2,128)(2,1)}, u32[]{:S(2)}, u32[]{:S(2)}) %all-to-all-start) | async-done | bytes 6291488 | tf_op jit(solution)/shard_map/all_to_all | solution.py:80
  365.2 6.9 %copy.56 = bf16[12,2,128,1024]{2,3,1,0:T(8,128)(2,1)} copy(bf16[12,2,128,1024]{2,1,0,3:T(2,128)(2,1)} %all-to-all-done) | data formatting | bytes 12582912 | tf_op jit(solution)/shard_map/all_to_all | solution.py:80
  372.1 8.7 %copy.57 = bf16[12,2,8,128,128]{4,3,2,1,0:T(8,128)(2,1)} copy(bf16[12,2,8,128,128]{3,4,2,1,0:T(8,128)(2,1)} %bitcast.114) | data formatting | bytes 12582912 | tf_op jit(solution)/shard_map/all_to_all | solution.py:80
  380.8 3.4 slice_bitcast_fusion
  384.2 1.2 copy-done
  385.4 0.4 fusion.41
  385.8 1.0 maximum_bitcast_fusion
  386.8 7.2 %bitcast_convert_fusion = bf16[4,3,256,2,4,128]{5,2,4,3,1,0:T(8,128)(2,1)} fusion(bf16[4,3,1,2,4,256,128]{6,5,3,4,2,1,0:T(8,128)(2,1)S(1)} %get-tuple-element.16, bf16[4,3,1,2,4,256,128]{6,5,3,4,2,1,0:T(8,128)(2,1)S(1)} %get-tuple-element.15, bf16[4,3,256,2,256,1,1]{4,3,2,1,0,6,5:T(2,128)(2,1)} %bitcast.119), kind=kOutput, calls=%fused_computation.6 | convolution fusion | flops 3249537024 | bytes 22020096 | tf_op jit(solution)/shard_map/pmorajc,pmkrj->pmocak/dot_general | solution.py:88
  393.9 8.6 %copy.62 = bf16[4,3,2,128,1024]{4,3,2,1,0:T(8,128)(2,1)} copy(bf16[4,3,2,128,1024]{3,4,2,1,0:T(8,128)(2,1)} %bitcast.118) | data formatting | bytes 12582912 | tf_op jit(solution)/shard_map/convert_element_type | solution.py:91
  (14 shorter events, 0.1 us)
Async XLA Ops:
  6.5 164.0 %all-gather.2.cloned.1.call-start = ((), (), s32[]{:S(2)}) async-start(), calls=%async_computation.1 | async-start | bytes 2359296 | tf_op jit(solution)/shard_map/all_gather | solution.py:57
  7.7 1.8 copy-start.3
  11.3 37.4 %collective-permute-start = (f32[1,3,256,512]{2,3,1,0:T(8,128)S(1)}, f32[1,3,256,512]{2,3,1,0:T(8,128)S(1)}, u32[]{:S(2)}, u32[]{:S(2)}) collective-permute-start(f32[1,3,256,512]{2,3,1,0:T(8,128)S(1)} %fusion.17), channel_id=1, source_target_pairs={{0,2},{2,0},{4,6},{6,4},{8,10},{10,8},{12,14},{14,12},{1,3},{3,1},... | collective-permute-start | bytes 4718600 | tf_op jit(solution)/shard_map/ppermute | solution.py:55
  48.9 35.6 %collective-permute-start.1 = (f32[1,3,256,512]{2,3,1,0:T(8,128)S(1)}, f32[1,3,256,512]{2,3,1,0:T(8,128)S(1)}, u32[]{:S(2)}, u32[]{:S(2)}) collective-permute-start(f32[1,3,256,512]{2,3,1,0:T(8,128)S(1)} %add.123), channel_id=1, source_target_pairs={{0,4},{2,6},{4,0},{6,2},{8,12},{10,14},{12,8},{14,10},{1,5},{3,7},... | collective-permute-start | bytes 4718600 | tf_op jit(solution)/shard_map/ppermute | solution.py:55
  84.8 69.4 %collective-permute-start.2 = (f32[1,3,256,512]{2,3,1,0:T(8,128)S(1)}, f32[1,3,256,512]{2,3,1,0:T(8,128)S(1)}, u32[]{:S(2)}, u32[]{:S(2)}) collective-permute-start(f32[1,3,256,512]{2,3,1,0:T(8,128)S(1)} %add.124), channel_id=1, source_target_pairs={{0,8},{2,10},{4,12},{6,14},{8,0},{10,2},{12,4},{14,6},{1,9},{3,11}... | collective-permute-start | bytes 4718600 | tf_op jit(solution)/shard_map/ppermute | solution.py:55
  162.9 4.8 %copy-start.4 = (s32[4,2]{0,1:T(2,128)S(1)}, s32[4,2]{0,1:T(2,128)}, u32[]{:S(2)}) copy-start(s32[4,2]{0,1:T(2,128)} %param.8) | copy-start | bytes 100
  162.9 4.8 %copy-start.2 = (bf16[4,1,128,4,256]{4,2,1,3,0:T(8,128)(2,1)S(1)}, bf16[4,1,128,4,256]{4,2,1,3,0:T(8,128)(2,1)}, u32[]{:S(2)}) copy-start(bf16[4,1,128,4,256]{4,2,1,3,0:T(8,128)(2,1)} %neg.44) | copy-start | bytes 3145732
  221.3 5.5 %copy-start.1 = (bf16[2,3,256,512]{3,2,1,0:T(8,128)(2,1)S(1)}, bf16[2,3,256,512]{3,2,1,0:T(8,128)(2,1)}, u32[]{:S(2)}) copy-start(bf16[2,3,256,512]{3,2,1,0:T(8,128)(2,1)} %all-gather.2.cloned.1.call-done) | copy-start | bytes 4718596
  221.3 143.9 %all-to-all-start = ((bf16[12,2,128,1024]{2,1,0,3:T(2,128)(2,1)}), bf16[12,2,128,1024]{2,1,0,3:T(2,128)(2,1)}, u32[]{:S(2)}, u32[]{:S(2)}) async-start(bf16[12,2,128,1024]{2,1,0,3:T(2,128)(2,1)} %copy.55), calls=%async_computation | async-start | bytes 12582912 | tf_op jit(solution)/shard_map/all_to_all | solution.py:80
  380.8 4.6 %copy-start = (bf16[12,2,8,128,128]{4,3,2,1,0:T(8,128)(2,1)S(1)}, bf16[12,2,8,128,128]{4,3,2,1,0:T(8,128)(2,1)}, u32[]{:S(2)}) copy-start(bf16[12,2,8,128,128]{4,3,2,1,0:T(8,128)(2,1)} %copy.57) | copy-start | bytes 18874372
Sparse Core Ops, SparseCore 0:
  155.8 10.6 all-gather.1
